TPU v7x, 256 devices: a whole 4x4x8 slice. The times are simulated.
256 devices in a mesh: row: 8 (over y, core), col: 32 (over z, x).
Axes of the slice: x: 4, y: 4, z: 8, core: 2. Of those that a mesh axis runs over, the one named last changes fastest.
Arguments:
- solution: float32 [8, 32, 16, 128, 128], P('row', 'col'), may hold values from -6 to 6
- residual: float32 [8, 32, 16, 128, 128], P('row', 'col'), may hold values from -6 to 6, as said below
- prev_direction: float32 [8, 32, 16, 128, 128], P('row', 'col'), may hold values from -6 to 6, as said below
- prev_dot: float32 [128], replicated, may hold values from 262144 to 1048576
- face_lists: int32 [8, 32, 4, 4], P('row', 'col'), may hold values from 0 to 16, as said below
- multiplicity: int32 [8, 32, 16], P('row', 'col'), may hold values from 1 to 2, as said below
- block_pattern: int32 [8, 32, 16, 3], P('row', 'col'), may hold values from 0 to 15, as said below
- schur: float32 [8, 32, 16, 3, 128, 128], P('row', 'col'), may hold values from -1 to 4, as said below
- neumann_inverse: float32 [8, 32, 16, 3, 128, 128], P('row', 'col'), may hold values from 0 to 2, as said below
- coarse_basis: float32 [8, 32, 8, 2048], P('row', 'col'), may hold values from -0.25 to 0.25
- primal_map: int32 [8, 32, 8], P('row', 'col'), may hold values from 0 to 1023, all different within a row
- coarse_inverse: float32 [1024, 1024], P('col'), may hold values from -1 to 1, as said below
Outputs:
- new_solution: float32 [8, 32, 16, 128, 128], P('row', 'col')
- new_residual: float32 [8, 32, 16, 128, 128], P('row', 'col')
- direction: float32 [8, 32, 16, 128, 128], P('row', 'col')
Inputs may be any that keep to these rules, and one draw needn't show every extreme that they name: face_lists[i, j, f, k] names the interface blocks that subdomain (i, j) shares with its neighbour across face f (0 toward row i-1, 1 toward row i+1, 2 toward column j-1, 3 toward column j+1); slot k of a face names the same unknowns as slot k of the neighbour's list for the facing face, and both lists have the same length, 1 to 4 blocks, none on faces at the grid's edge; unused slots hold 16; no block lies on two faces; some face holds 4 blocks. multiplicity is 2 for blocks named in face_lists and 1 for the others. block_pattern[i, j, b, 0] = b; the two other entries of block row b are two other blocks, each of which lists b in turn. `schur`: each subdomain's Schur complement is symmetric positive definite, with positive diagonal and no positive entry off it. `neumann_inverse`: each subdomain's local solve matrix is symmetric positive definite. `coarse_inverse`: symmetric positive definite. `residual`: copies of an unknown held by two subdomains (slot k of facing lists) are equal. `prev_direction`: copies of an unknown held by two subdomains (slot k of facing lists) are equal.
All inputs are finite; a program needn't handle non-finite values.
Results may differ from a plain program's by a relative error of at most 0.0003.
Values sent between devices are 32-bit elements; how exact they have to be, the bound alone decides.
A program may use at most 128 MiB of HBM per device.

v0:
```python
import jax
import jax.numpy as jnp
from jax import lax
from jax.sharding import PartitionSpec as P

HIGH = lax.Precision.HIGHEST


def extended(cells, sides, width):
    for axis, dim in sides:
        count = lax.axis_size(axis)
        ends = count - 1
        head = lax.slice_in_dim(cells, 0, width, axis=dim)
        tail = lax.slice_in_dim(cells, cells.shape[dim] - width, cells.shape[dim], axis=dim)
        cells = jnp.concatenate(
            [
                lax.ppermute(tail, axis, [(i, (i + 1) % count) for i in range(ends)]),
                cells,
                lax.ppermute(head, axis, [((i + 1) % count, i) for i in range(ends)]),
            ],
            axis=dim,
        )
    return cells


def block_product(blocks, pattern, values_in):
    stacked_count, block_count, dofs, cases = values_in.shape
    gathered = jnp.take(values_in, pattern.reshape(-1), axis=1)
    gathered = gathered.reshape(stacked_count, block_count, pattern.shape[1], dofs, cases)
    return jnp.einsum("bkij,vbkjn->vbin", blocks, gathered, precision=HIGH)


def assemble(values_in, faces):
    stacked_count, block_count, dofs, cases = values_in.shape
    flattened = values_in.reshape(stacked_count, block_count, dofs * cases)
    indicator = (faces[..., None] == jnp.arange(block_count)).astype(jnp.float32)
    face_values = jnp.einsum("fkb,vbc->fvkc", indicator, flattened, precision=HIGH)
    row_faces = extended(face_values[0:2], (("row", 0),), 1)
    col_faces = extended(face_values[2:4], (("col", 0),), 1)
    received = jnp.stack([row_faces[0], row_faces[3], col_faces[0], col_faces[3]])
    added = jnp.einsum("fkb,fvkc->vbc", indicator, received, precision=HIGH)
    return (flattened + added).reshape(values_in.shape)


def precondition(residual, weight, faces, pattern, neumann, basis, primal_map, inverse_rows):
    scaled = residual * weight
    local_term = block_product(neumann, pattern, scaled[None])[0]
    cases = residual.shape[-1]
    coarse_local = jnp.dot(basis, scaled.reshape(-1, cases), precision=HIGH)
    owned_count, coarse_total_rows = inverse_rows.shape
    indicator = (primal_map[:, None] == jnp.arange(coarse_total_rows)).astype(jnp.float32)
    owned_rhs = lax.psum_scatter(
        jnp.dot(indicator.T, coarse_local, precision=HIGH), "col", scatter_dimension=0, tiled=True
    )
    owned_rhs = lax.psum(owned_rhs, "row")
    columns = inverse_rows
    owned_solution = jnp.dot(
        columns, lax.all_gather(owned_rhs, "col", axis=0, tiled=True), precision=HIGH
    )
    columns = indicator
    own_coarse = jnp.dot(
        columns, lax.all_gather(owned_solution, "col", axis=0, tiled=True), precision=HIGH
    )
    coarse_back = jnp.dot(basis.T, own_coarse, precision=HIGH).reshape(residual.shape)
    return assemble(((local_term + coarse_back) * weight)[None], faces)[0]


def per_device(
    solution,
    residual,
    prev_direction,
    prev_dot,
    face_lists,
    multiplicity,
    block_pattern,
    schur,
    neumann_inverse,
    coarse_basis,
    primal_map,
    coarse_inverse,
):
    faces = face_lists[0, 0]
    pattern = block_pattern[0, 0]
    weight = (1.0 / multiplicity[0, 0].astype(jnp.float32))[:, None, None]
    current = residual[0, 0]
    previous = prev_direction[0, 0]
    precond = precondition(
        current,
        weight,
        faces,
        pattern,
        neumann_inverse[0, 0],
        coarse_basis[0, 0],
        primal_map[0, 0],
        coarse_inverse,
    )
    local_precond_dot = jnp.sum(current * precond * weight, axis=(0, 1))
    precond_dot = lax.psum(local_precond_dot, ("row", "col"))
    direction_mix = precond_dot / prev_dot
    direction = precond + direction_mix * previous
    image = assemble(block_product(schur[0, 0], pattern, direction[None]), faces)[0]
    curvature = lax.psum(jnp.sum(direction * image * weight, axis=(0, 1)), ("row", "col"))
    step_size = precond_dot / curvature
    new_solution = solution[0, 0] + step_size * direction
    new_residual = current - step_size * image
    return (new_solution[None, None], new_residual[None, None], direction[None, None])


def solution(mesh):
    placed = (
        P("row", "col", None, None, None),
        P("row", "col", None, None, None),
        P("row", "col", None, None, None),
        P(),
        P("row", "col", None, None),
        P("row", "col", None),
        P("row", "col", None, None),
        P("row", "col", None, None, None, None),
        P("row", "col", None, None, None, None),
        P("row", "col", None, None),
        P("row", "col", None),
        P("col", None),
    )
    return jax.shard_map(
        per_device,
        mesh=mesh,
        in_specs=placed,
        out_specs=(
            P("row", "col", None, None, None),
            P("row", "col", None, None, None),
            P("row", "col", None, None, None),
        ),
        check_vma=False,
    )
```

profile of v0, /device:TPU:1, one launch (start us, length us, event | category | flops | bytes accessed | tf_op | source)
XLA Modules:
  0.0 597.9 jit_solution(11276702184320067996)
XLA Ops:
  12.5 2.3 fusion.31
  15.1 3.6 gather_fusion
  20.9 6.2 %fusion.6 = f32[1,16,128,128]{2,3,1,0:T(8,128)} fusion(f32[16,3,128,128]{3,2,1,0:T(8,128)S(1)} %bitcast.147, f32[1,1,16,3,128,128]{5,4,3,2,1,0:T(8,128)S(1)} %copy-done), kind=kOutput, calls=%fused_computation.15 | convolution fusion | flops 1207959552 | bytes 7340032 | tf_op jit(solution)/shard_map/bkij,vbkjn->vbin/dot_general | solution.py:30
  27.1 2.6 copy.44
  29.7 194.6 %reduce-scatter.2.cloned.1.call-done = f32[32,128]{1,0:T(8,128)} async-done(((f32[1024,128]{1,0:T(8,128)}), f32[32,128]{1,0:T(8,128)}) %reduce-scatter.2.cloned.1.call-update) | async-done | bytes 16400 | tf_op jit(solution)/shard_map/reduce_scatter | solution.py:52
  224.3 26.4 %psum.21 = f32[32,128]{1,0:T(8,128)S(1)} all-reduce(f32[32,128]{1,0:T(8,128)} %reduce-scatter.2.cloned.1.call-done), channel_id=1, replica_groups=mesh['row'=8,'col'=32] {'row'}, use_global_device_ids=true, to_apply=%region_1.3 | all-reduce | flops 4096 | bytes 32768 | tf_op jit(solution)/shard_map/psum | solution.py:55
  250.7 35.9 %all_gather.6 = f32[1024,128]{1,0:T(8,128)S(1)} all-gather(f32[32,128]{1,0:T(8,128)S(1)} %psum.21), channel_id=1, replica_groups=mesh['row'=8,'col'=32] {'col'}, dimensions={0}, use_global_device_ids=true | all-gather | bytes 540672 | tf_op jit(solution)/shard_map/all_gather | solution.py:58
  287.0 35.8 %all_gather.7 = f32[1024,128]{1,0:T(8,128)S(1)} all-gather(f32[32,128]{1,0:T(8,128)S(1)} %convolution_bitcast_fusion.5), channel_id=1, replica_groups=mesh['row'=8,'col'=32] {'col'}, dimensions={0}, use_global_device_ids=true | all-gather | bytes 540672 | tf_op jit(solution)/shard_map/all_gather | solution.py:62
  325.0 2.5 copy.42
  327.6 2.4 reshape.184
  329.9 3.0 convolution_bitcast_fusion.3
  333.9 27.6 %collective-permute-start = (f32[1,1,4,16384]{3,2,0,1:T(4,128)}, f32[1,1,4,16384]{3,2,0,1:T(4,128)}, u32[]{:S(2)}, u32[]{:S(2)}) collective-permute-start(f32[1,1,4,16384]{3,2,0,1:T(4,128)} %get-tuple-element.10), channel_id=1, source_target_pairs={{0,32},{32,64},{64,96},{96,128},{128,160},{160,192},{192,224},{1,3... | collective-permute-start | bytes 786440 | tf_op jit(solution)/shard_map/ppermute | solution.py:17
  361.5 3.8 collective-permute-start.1
  365.4 3.1 collective-permute-start.2
  369.7 2.5 copy.41
  372.2 2.4 squeeze.32
  374.6 2.4 reshape.183
  378.6 3.4 fusion.1
  384.5 78.4 %psum.22 = f32[128]{0:T(128)S(1)} all-reduce(f32[128]{0:T(128)S(1)} %fusion.14), channel_id=1, replica_groups=mesh['row'=8,'col'=32] {'row','col'}, use_global_device_ids=true, to_apply=%region_3.5 | all-reduce | flops 128 | bytes 1024 | tf_op jit(solution)/shard_map/psum | solution.py:98
  462.9 2.7 fusion.12
  465.5 3.6 gather_fusion.1
  469.1 2.3 bitcast_select_fusion
  472.0 6.3 %fusion.9 = f32[1,16,128,128]{2,3,1,0:T(8,128)} fusion(f32[16,3,128,128]{3,2,1,0:T(8,128)S(1)} %bitcast.146, f32[1,1,16,3,128,128]{5,4,3,2,1,0:T(8,128)S(1)} %copy-done.7), kind=kOutput, calls=%fused_computation.16 | convolution fusion | flops 1207959552 | bytes 7340032 | tf_op jit(solution)/shard_map/bkij,vbkjn->vbin/dot_general | solution.py:30
  478.3 2.5 copy.47
  480.8 2.4 reshape.224
  483.2 2.4 reshape.187
  485.6 2.4 convolution_bitcast_fusion.1
  488.1 3.7 collective-permute-start.4
  497.0 2.5 collective-permute-done.5
  501.7 4.1 collective-permute-done.7
  508.2 78.4 %psum.23 = f32[128]{0:T(128)S(1)} all-reduce(f32[128]{0:T(128)S(1)} %bitcast_reduce_fusion), channel_id=1, replica_groups=mesh['row'=8,'col'=32] {'row','col'}, use_global_device_ids=true, to_apply=%region_6.8 | all-reduce | flops 128 | bytes 1024 | tf_op jit(solution)/shard_map/psum | solution.py:102
  586.6 4.5 multiply_add_fusion
  (63 shorter events, 27.0 us)
Async XLA Ops:
  7.2 13.7 %copy-start = (f32[1,1,16,3,128,128]{5,4,3,2,1,0:T(8,128)S(1)}, f32[1,1,16,3,128,128]{5,4,3,2,1,0:T(8,128)}, u32[]{:S(2)}) copy-start(f32[1,1,16,3,128,128]{5,4,3,2,1,0:T(8,128)} %param.22) | copy-start | bytes 9437188
  7.2 3.8 copy-start.11
  7.2 217.1 %reduce-scatter.2.cloned.1.call-start = ((), (), s32[]{:S(2)}) async-start(), calls=%async_computation.1 | async-start | bytes 540672 | tf_op jit(solution)/shard_map/reduce_scatter | solution.py:52
  8.0 6.8 %copy-start.12 = (s32[1,1,16,3]{2,1,3,0:T(1,128)S(1)}, s32[1,1,16,3]{2,1,3,0:T(1,128)}, u32[]{:S(2)}) copy-start(s32[1,1,16,3]{2,1,3,0:T(1,128)} %param.20) | copy-start | bytes 580
  20.9 265.7 %copy-start.9 = (f32[32,1024]{1,0:T(8,128)S(1)}, f32[32,1024]{1,0:T(8,128)}, u32[]{:S(2)}) copy-start(f32[32,1024]{1,0:T(8,128)} %param.25) | copy-start | bytes 393220
  27.1 295.9 %copy-start.8 = (f32[1,1,8,2048]{3,2,1,0:T(8,128)S(1)}, f32[1,1,8,2048]{3,2,1,0:T(8,128)}, u32[]{:S(2)}) copy-start(f32[1,1,8,2048]{3,2,1,0:T(8,128)} %param.23) | copy-start | bytes 196612
  286.9 43.0 %copy-start.10 = (s32[1,1,4,4]{3,2,1,0:T(4,128)S(1)}, s32[1,1,4,4]{3,2,1,0:T(4,128)}, u32[]{:S(2)}) copy-start(s32[1,1,4,4]{3,2,1,0:T(4,128)} %param.18) | copy-start | bytes 196
  333.9 43.1 %collective-permute-start = (f32[1,1,4,16384]{3,2,0,1:T(4,128)}, f32[1,1,4,16384]{3,2,0,1:T(4,128)}, u32[]{:S(2)}, u32[]{:S(2)}) collective-permute-start(f32[1,1,4,16384]{3,2,0,1:T(4,128)} %get-tuple-element.10), channel_id=1, source_target_pairs={{0,32},{32,64},{64,96},{96,128},{128,160},{160,192},{192,224},{1,3... | collective-permute-start | bytes 786440 | tf_op jit(solution)/shard_map/ppermute | solution.py:17
  361.5 15.5 %collective-permute-start.1 = (f32[1,1,4,16384]{3,2,0,1:T(4,128)}, f32[1,1,4,16384]{3,2,0,1:T(4,128)}, u32[]{:S(2)}, u32[]{:S(2)}) collective-permute-start(f32[1,1,4,16384]{3,2,0,1:T(4,128)} %get-tuple-element.13), channel_id=1, source_target_pairs={{32,0},{64,32},{96,64},{128,96},{160,128},{192,160},{224,192},{33,... | collective-permute-start | bytes 786440 | tf_op jit(solution)/shard_map/ppermute | solution.py:19
  365.4 11.7 %collective-permute-start.2 = (f32[1,1,4,16384]{3,2,0,1:T(4,128)}, f32[1,1,4,16384]{3,2,0,1:T(4,128)}, u32[]{:S(2)}, u32[]{:S(2)}) collective-permute-start(f32[1,1,4,16384]{3,2,0,1:T(4,128)} %get-tuple-element.12), channel_id=1, source_target_pairs={{0,1},{1,2},{2,3},{3,4},{4,5},{5,6},{6,7},{7,8},{8,9},{9,10},{10,1... | collective-permute-start | bytes 786440 | tf_op jit(solution)/shard_map/ppermute | solution.py:17
  368.4 10.2 %collective-permute-start.3 = (f32[1,1,4,16384]{3,2,0,1:T(4,128)S(1)}, f32[1,1,4,16384]{3,2,0,1:T(4,128)}, u32[]{:S(2)}, u32[]{:S(2)}) collective-permute-start(f32[1,1,4,16384]{3,2,0,1:T(4,128)S(1)} %get-tuple-element.11), channel_id=1, source_target_pairs={{1,0},{2,1},{3,2},{4,3},{5,4},{6,5},{7,6},{8,7},{9,8},{10,9},{11,1... | collective-permute-start | bytes 786440 | tf_op jit(solution)/shard_map/ppermute | solution.py:19
  378.6 5.5 copy-start.1
  382.0 1.0 copy-start.4
  382.0 80.9 %copy-start.13 = (f32[128]{0:T(128)S(1)}, f32[128]{0:T(128)}, u32[]{:S(2)}) copy-start(f32[128]{0:T(128)} %param.17) | copy-start | bytes 1540
  383.2 1.0 copy-start.2
  469.1 2.8 copy-start.7
  485.6 20.1 %copy-start.3 = (f32[1,16,16384]{2,1,0:T(8,128)S(1)}, f32[1,16,16384]{2,1,0:T(8,128)}, u32[]{:S(2)}) copy-start(f32[1,16,16384]{2,1,0:T(8,128)} %squeeze.32) | copy-start | bytes 3145732
  485.6 20.1 %copy-start.5 = (f32[1,16,16384]{2,1,0:T(8,128)S(1)}, f32[1,16,16384]{2,1,0:T(8,128)}, u32[]{:S(2)}) copy-start(f32[1,16,16384]{2,1,0:T(8,128)} %copy-done.4) | copy-start | bytes 3145732
  485.6 20.1 %copy-start.6 = (f32[1,16,16384]{2,1,0:T(8,128)S(1)}, f32[1,16,16384]{2,1,0:T(8,128)}, u32[]{:S(2)}) copy-start(f32[1,16,16384]{2,1,0:T(8,128)} %reshape.187) | copy-start | bytes 3145732
  488.1 8.9 %collective-permute-start.4 = (f32[1,1,4,16384]{3,2,0,1:T(4,128)S(1)}, f32[1,1,4,16384]{3,2,0,1:T(4,128)S(1)}, u32[]{:S(2)}, u32[]{:S(2)}) collective-permute-start(f32[1,1,4,16384]{3,2,0,1:T(4,128)S(1)} %get-tuple-element.6), channel_id=1, source_target_pairs={{0,32},{32,64},{64,96},{96,128},{128,160},{160,192},{192,224},{1,3... | collective-permute-start | bytes 786440 | tf_op jit(solution)/shard_map/ppermute | solution.py:17
  491.8 7.7 %collective-permute-start.5 = (f32[1,1,4,16384]{3,2,0,1:T(4,128)S(1)}, f32[1,1,4,16384]{3,2,0,1:T(4,128)S(1)}, u32[]{:S(2)}, u32[]{:S(2)}) collective-permute-start(f32[1,1,4,16384]{3,2,0,1:T(4,128)S(1)} %get-tuple-element.9), channel_id=1, source_target_pairs={{32,0},{64,32},{96,64},{128,96},{160,128},{192,160},{224,192},{33,... | collective-permute-start | bytes 786440 | tf_op jit(solution)/shard_map/ppermute | solution.py:19
  493.7 7.9 %collective-permute-start.6 = (f32[1,1,4,16384]{3,2,0,1:T(4,128)S(1)}, f32[1,1,4,16384]{3,2,0,1:T(4,128)S(1)}, u32[]{:S(2)}, u32[]{:S(2)}) collective-permute-start(f32[1,1,4,16384]{3,2,0,1:T(4,128)S(1)} %get-tuple-element.8), channel_id=1, source_target_pairs={{0,1},{1,2},{2,3},{3,4},{4,5},{5,6},{6,7},{7,8},{8,9},{9,10},{10,1... | collective-permute-start | bytes 786440 | tf_op jit(solution)/shard_map/ppermute | solution.py:17
  495.7 10.1 %collective-permute-start.7 = (f32[1,1,4,16384]{3,2,0,1:T(4,128)S(1)}, f32[1,1,4,16384]{3,2,0,1:T(4,128)S(1)}, u32[]{:S(2)}, u32[]{:S(2)}) collective-permute-start(f32[1,1,4,16384]{3,2,0,1:T(4,128)S(1)} %get-tuple-element.7), channel_id=1, source_target_pairs={{1,0},{2,1},{3,2},{4,3},{5,4},{6,5},{7,6},{8,7},{9,8},{10,9},{11,1... | collective-permute-start | bytes 786440 | tf_op jit(solution)/shard_map/ppermute | solution.py:19
Sparse Core Ops, SparseCore 0:
  12.7 211.5 reduce-scatter.1
where the time goes:
time: 599 us; the launch traced here: 598 us
  blocking collectives  255 us (43%)
  waiting for transfers between devices  205 us (34%)
  starting transfers between devices  44.6 us (7%)
  local copies, waits for them, and re-layouts  34.4 us (6%)
  matrix products  28.1 us (5%)
  other arithmetic  16.6 us (3%)
  between operations  14.3 us (2%)
    reduce_scatter x1, waiting for transfers between devices, precondition(): lax.psum_scatter(jnp.dot(indicator.T, coarse_local, precision=HIGH), 'col...  195 us
    psum x1, blocking collectives, per_device(): lax.psum(jnp.sum(direction * image * weight, axis=(0, 1)), ('row', 'col'))  78.4 us
    psum x1, blocking collectives, per_device(): precond_dot = lax.psum(local_precond_dot, ('row', 'col'))  78.4 us
    ppermute x4, starting transfers between devices, extended(): lax.ppermute(tail, axis, [(i, (i + 1) % count) for i in range(ends)])  36.3 us
    all_gather x1, blocking collectives, precondition(): lax.all_gather(owned_rhs, 'col', axis=0, tiled=True)  35.9 us
    all_gather x1, blocking collectives, precondition(): lax.all_gather(owned_solution, 'col', axis=0, tiled=True)  35.8 us
    psum x1, blocking collectives, precondition(): owned_rhs = lax.psum(owned_rhs, 'row')  26.4 us
    dot_general x2, matrix products, block_product(): return jnp.einsum('bkij,vbkjn->vbin', blocks, gathered, precision=HIGH)  12.5 us
  transfers between devices with their start and end apart: 9, of which 5 were waited for; matrix products, arithmetic and copies ran while one was open for 4% of the time, Pallas kernels for 0%

commit v1 on v0

--- a/solution.py
+++ b/solution.py
@@ -2,6 +2,7 @@
 import jax.numpy as jnp
 from jax import lax
 from jax.sharding import PartitionSpec as P
+from jax.lax import all_to_all, axis_size
 
 HIGH = lax.Precision.HIGHEST
 
@@ -59,7 +60,17 @@
     )
     columns = indicator
     own_coarse = jnp.dot(
-        columns, lax.all_gather(owned_solution, "col", axis=0, tiled=True), precision=HIGH
+        columns,
+        jnp.concatenate(
+            all_to_all(
+                jnp.stack([owned_solution for _ in range(axis_size("col"))], axis=0),
+                axis_name="col",
+                split_axis=0,
+                concat_axis=0,
+            ),
+            axis=0,
+        ),
+        precision=HIGH,
     )
     coarse_back = jnp.dot(basis.T, own_coarse, precision=HIGH).reshape(residual.shape)
     return assemble(((local_term + coarse_back) * weight)[None], faces)[0]

time: 599 us -> 574 us (0.958)
  blocking collectives: 255 us -> 218 us
  waiting for transfers between devices: 205 us -> 218 us
    all_gather x1 -> x0, blocking collectives: 35.8 us -> none  [precondition(): lax.all_gather(owned_solution, 'col', axis=0, tiled=True)]
    reduce_scatter x1, waiting for transfers between devices: 195 us -> 206 us  [precondition(): lax.psum_scatter(jnp.dot(indicator.T, coarse_local, precision=HIGH), 'col...]
    ppermute x4, starting transfers between devices: 36.3 us -> 26.1 us  [extended(): lax.ppermute(tail, axis, [(i, (i + 1) % count) for i in range(ends)])]
    all_to_all x0 -> x1, starting transfers between devices: none -> 7.09 us  [precondition(): all_to_all(jnp.stack([owned_solution for _ in range(axis_size('col'))], a...]
  transfers between devices with their start and end apart: 9 -> 10, of which waited for: 5 -> 6; matrix products, arithmetic and copies ran while one was open for 4% -> 4% of each run, Pallas kernels for 0% -> 0%
where the time goes in v1:
time: 574 us; the launch traced here: 573 us
  waiting for transfers between devices  218 us (38%)
  blocking collectives  218 us (38%)
  starting transfers between devices  42.5 us (7%)
  local copies, waits for them, and re-layouts  35.3 us (6%)
  matrix products  29.2 us (5%)
  other arithmetic  16.6 us (3%)
  between operations  14.3 us (2%)
    reduce_scatter x1, waiting for transfers between devices, precondition(): lax.psum_scatter(jnp.dot(indicator.T, coarse_local, precision=HIGH), 'col...  206 us
    psum x1, blocking collectives, per_device(): lax.psum(jnp.sum(direction * image * weight, axis=(0, 1)), ('row', 'col'))  78.4 us
    psum x1, blocking collectives, per_device(): precond_dot = lax.psum(local_precond_dot, ('row', 'col'))  76.9 us
    all_gather x1, blocking collectives, precondition(): lax.all_gather(owned_rhs, 'col', axis=0, tiled=True)  35.9 us
    psum x1, blocking collectives, precondition(): owned_rhs = lax.psum(owned_rhs, 'row')  26.4 us
    ppermute x4, starting transfers between devices, extended(): lax.ppermute(tail, axis, [(i, (i + 1) % count) for i in range(ends)])  26.1 us
    dot_general x2, matrix products, block_product(): return jnp.einsum('bkij,vbkjn->vbin', blocks, gathered, precision=HIGH)  12.5 us
  transfers between devices with their start and end apart: 10, of which 6 were waited for; matrix products, arithmetic and copies ran while one was open for 4% of the time, Pallas kernels for 0%

profile of v1, /device:TPU:1, one launch (start us, length us, event | category | flops | bytes accessed | tf_op | source)
XLA Modules:
  0.0 573.1 jit_solution(7170802521336095004)
XLA Ops:
  12.7 2.3 fusion.31
  15.1 3.6 gather_fusion
  18.7 205.6 %reduce-scatter.2.cloned.1.call-done = f32[32,128]{1,0:T(8,128)} async-done(((f32[1024,128]{1,0:T(8,128)}), f32[32,128]{1,0:T(8,128)}) %reduce-scatter.2.cloned.1.call-update) | async-done | bytes 16400 | tf_op jit(solution)/shard_map/reduce_scatter | solution.py:53
  224.3 26.4 %psum.21 = f32[32,128]{1,0:T(8,128)S(1)} all-reduce(f32[32,128]{1,0:T(8,128)} %reduce-scatter.2.cloned.1.call-done), channel_id=1, replica_groups=mesh['row'=8,'col'=32] {'row'}, use_global_device_ids=true, to_apply=%region_1.3 | all-reduce | flops 4096 | bytes 32768 | tf_op jit(solution)/shard_map/psum | solution.py:56
  250.7 35.9 %all_gather.3 = f32[1024,128]{1,0:T(8,128)S(1)} all-gather(f32[32,128]{1,0:T(8,128)S(1)} %psum.21), channel_id=1, replica_groups=mesh['row'=8,'col'=32] {'col'}, dimensions={0}, use_global_device_ids=true | all-gather | bytes 540672 | tf_op jit(solution)/shard_map/all_gather | solution.py:59
  287.8 7.1 %all-to-all-start = ((f32[32,32,128]{2,1,0:T(8,128)}), f32[32,32,128]{2,1,0:T(8,128)}, u32[]{:S(2)}, u32[]{:S(2)}) async-start(f32[32,32,128]{2,1,0:T(8,128)} %stack.6), calls=%async_computation.1 | async-start | bytes 1048576 | tf_op jit(solution)/shard_map/all_to_all | solution.py:65
  297.1 6.2 %fusion.6 = f32[1,16,128,128]{2,3,1,0:T(8,128)} fusion(f32[16,3,128,128]{3,2,1,0:T(8,128)S(1)} %bitcast.148, f32[1,1,16,3,128,128]{5,4,3,2,1,0:T(8,128)S(1)} %copy-done), kind=kOutput, calls=%fused_computation.15 | convolution fusion | flops 1207959552 | bytes 7340032 | tf_op jit(solution)/shard_map/bkij,vbkjn->vbin/dot_general | solution.py:31
  303.3 2.5 copy.34
  310.9 2.5 copy.32
  313.5 2.4 reshape.190
  315.8 3.0 convolution_bitcast_fusion.3
  319.8 17.5 %collective-permute-start = (f32[1,1,4,16384]{3,2,0,1:T(4,128)}, f32[1,1,4,16384]{3,2,0,1:T(4,128)}, u32[]{:S(2)}, u32[]{:S(2)}) collective-permute-start(f32[1,1,4,16384]{3,2,0,1:T(4,128)} %get-tuple-element.10), channel_id=1, source_target_pairs={{0,32},{32,64},{64,96},{96,128},{128,160},{160,192},{192,224},{1,3... | collective-permute-start | bytes 786440 | tf_op jit(solution)/shard_map/ppermute | solution.py:18
  337.4 4.8 collective-permute-start.1
  342.2 2.9 collective-permute-start.2
  346.4 2.5 copy.31
  349.0 2.4 squeeze.32
  351.4 2.4 reshape.189
  355.3 3.4 fusion.1
  361.2 76.9 %psum.22 = f32[128]{0:T(128)S(1)} all-reduce(f32[128]{0:T(128)S(1)} %fusion.14), channel_id=1, replica_groups=mesh['row'=8,'col'=32] {'row','col'}, use_global_device_ids=true, to_apply=%region_3.5 | all-reduce | flops 128 | bytes 1024 | tf_op jit(solution)/shard_map/psum | solution.py:109
  438.1 2.7 fusion.12
  440.8 3.6 gather_fusion.1
  444.4 2.3 bitcast_select_fusion
  447.2 6.3 %fusion.9 = f32[1,16,128,128]{2,3,1,0:T(8,128)} fusion(f32[16,3,128,128]{3,2,1,0:T(8,128)S(1)} %bitcast.147, f32[1,1,16,3,128,128]{5,4,3,2,1,0:T(8,128)S(1)} %copy-done.7), kind=kOutput, calls=%fused_computation.16 | convolution fusion | flops 1207959552 | bytes 7340032 | tf_op jit(solution)/shard_map/bkij,vbkjn->vbin/dot_general | solution.py:31
  453.5 2.5 copy.37
  456.0 2.4 reshape.230
  458.4 2.4 reshape.193
  460.9 2.4 convolution_bitcast_fusion.1
  463.4 3.7 collective-permute-start.4
  472.2 2.5 collective-permute-done.5
  476.9 4.1 collective-permute-done.7
  483.4 78.4 %psum.23 = f32[128]{0:T(128)S(1)} all-reduce(f32[128]{0:T(128)S(1)} %bitcast_reduce_fusion), channel_id=1, replica_groups=mesh['row'=8,'col'=32] {'row','col'}, use_global_device_ids=true, to_apply=%region_6.8 | all-reduce | flops 128 | bytes 1024 | tf_op jit(solution)/shard_map/psum | solution.py:113
  561.8 4.5 multiply_add_fusion
  (65 shorter events, 30.6 us)
Async XLA Ops:
  7.2 289.9 %copy-start = (f32[1,1,16,3,128,128]{5,4,3,2,1,0:T(8,128)S(1)}, f32[1,1,16,3,128,128]{5,4,3,2,1,0:T(8,128)}, u32[]{:S(2)}) copy-start(f32[1,1,16,3,128,128]{5,4,3,2,1,0:T(8,128)} %param.22) | copy-start | bytes 9437188
  7.2 3.8 copy-start.11
  7.2 5.3 copy-start.12
  7.2 217.1 %reduce-scatter.2.cloned.1.call-start = ((), (), s32[]{:S(2)}) async-start(), calls=%async_computation.2 | async-start | bytes 540672 | tf_op jit(solution)/shard_map/reduce_scatter | solution.py:53
  15.1 271.4 %copy-start.9 = (f32[32,1024]{1,0:T(8,128)S(1)}, f32[32,1024]{1,0:T(8,128)}, u32[]{:S(2)}) copy-start(f32[32,1024]{1,0:T(8,128)} %param.25) | copy-start | bytes 393220
  287.8 19.8 %all-to-all-start = ((f32[32,32,128]{2,1,0:T(8,128)}), f32[32,32,128]{2,1,0:T(8,128)}, u32[]{:S(2)}, u32[]{:S(2)}) async-start(f32[32,32,128]{2,1,0:T(8,128)} %stack.6), calls=%async_computation.1 | async-start | bytes 1048576 | tf_op jit(solution)/shard_map/all_to_all | solution.py:65
  297.1 11.9 %copy-start.8 = (f32[1,1,8,2048]{3,2,1,0:T(8,128)S(1)}, f32[1,1,8,2048]{3,2,1,0:T(8,128)}, u32[]{:S(2)}) copy-start(f32[1,1,8,2048]{3,2,1,0:T(8,128)} %param.23) | copy-start | bytes 196612
  305.9 10.0 %copy-start.10 = (s32[1,1,4,4]{3,2,1,0:T(4,128)S(1)}, s32[1,1,4,4]{3,2,1,0:T(4,128)}, u32[]{:S(2)}) copy-start(s32[1,1,4,4]{3,2,1,0:T(4,128)} %param.18) | copy-start | bytes 196
  319.8 33.9 %collective-permute-start = (f32[1,1,4,16384]{3,2,0,1:T(4,128)}, f32[1,1,4,16384]{3,2,0,1:T(4,128)}, u32[]{:S(2)}, u32[]{:S(2)}) collective-permute-start(f32[1,1,4,16384]{3,2,0,1:T(4,128)} %get-tuple-element.10), channel_id=1, source_target_pairs={{0,32},{32,64},{64,96},{96,128},{128,160},{160,192},{192,224},{1,3... | collective-permute-start | bytes 786440 | tf_op jit(solution)/shard_map/ppermute | solution.py:18
  337.4 16.4 %collective-permute-start.1 = (f32[1,1,4,16384]{3,2,0,1:T(4,128)}, f32[1,1,4,16384]{3,2,0,1:T(4,128)}, u32[]{:S(2)}, u32[]{:S(2)}) collective-permute-start(f32[1,1,4,16384]{3,2,0,1:T(4,128)} %get-tuple-element.13), channel_id=1, source_target_pairs={{32,0},{64,32},{96,64},{128,96},{160,128},{192,160},{224,192},{33,... | collective-permute-start | bytes 786440 | tf_op jit(solution)/shard_map/ppermute | solution.py:20
  342.2 11.5 %collective-permute-start.2 = (f32[1,1,4,16384]{3,2,0,1:T(4,128)}, f32[1,1,4,16384]{3,2,0,1:T(4,128)}, u32[]{:S(2)}, u32[]{:S(2)}) collective-permute-start(f32[1,1,4,16384]{3,2,0,1:T(4,128)} %get-tuple-element.12), channel_id=1, source_target_pairs={{0,1},{1,2},{2,3},{3,4},{4,5},{5,6},{6,7},{7,8},{8,9},{9,10},{10,1... | collective-permute-start | bytes 786440 | tf_op jit(solution)/shard_map/ppermute | solution.py:18
  345.2 10.2 %collective-permute-start.3 = (f32[1,1,4,16384]{3,2,0,1:T(4,128)S(1)}, f32[1,1,4,16384]{3,2,0,1:T(4,128)}, u32[]{:S(2)}, u32[]{:S(2)}) collective-permute-start(f32[1,1,4,16384]{3,2,0,1:T(4,128)S(1)} %get-tuple-element.11), channel_id=1, source_target_pairs={{1,0},{2,1},{3,2},{4,3},{5,4},{6,5},{7,6},{8,7},{9,8},{10,9},{11,1... | collective-permute-start | bytes 786440 | tf_op jit(solution)/shard_map/ppermute | solution.py:20
  355.3 5.5 copy-start.1
  358.7 1.0 copy-start.4
  358.7 79.4 %copy-start.13 = (f32[128]{0:T(128)S(1)}, f32[128]{0:T(128)}, u32[]{:S(2)}) copy-start(f32[128]{0:T(128)} %param.17) | copy-start | bytes 1540
  359.9 1.0 copy-start.2
  444.4 2.8 copy-start.7
  460.9 20.1 %copy-start.3 = (f32[1,16,16384]{2,1,0:T(8,128)S(1)}, f32[1,16,16384]{2,1,0:T(8,128)}, u32[]{:S(2)}) copy-start(f32[1,16,16384]{2,1,0:T(8,128)} %squeeze.32) | copy-start | bytes 3145732
  460.9 20.1 %copy-start.5 = (f32[1,16,16384]{2,1,0:T(8,128)S(1)}, f32[1,16,16384]{2,1,0:T(8,128)}, u32[]{:S(2)}) copy-start(f32[1,16,16384]{2,1,0:T(8,128)} %copy-done.4) | copy-start | bytes 3145732
  460.9 20.1 %copy-start.6 = (f32[1,16,16384]{2,1,0:T(8,128)S(1)}, f32[1,16,16384]{2,1,0:T(8,128)}, u32[]{:S(2)}) copy-start(f32[1,16,16384]{2,1,0:T(8,128)} %reshape.193) | copy-start | bytes 3145732
  463.4 8.8 %collective-permute-start.4 = (f32[1,1,4,16384]{3,2,0,1:T(4,128)S(1)}, f32[1,1,4,16384]{3,2,0,1:T(4,128)S(1)}, u32[]{:S(2)}, u32[]{:S(2)}) collective-permute-start(f32[1,1,4,16384]{3,2,0,1:T(4,128)S(1)} %get-tuple-element.6), channel_id=1, source_target_pairs={{0,32},{32,64},{64,96},{96,128},{128,160},{160,192},{192,224},{1,3... | collective-permute-start | bytes 786440 | tf_op jit(solution)/shard_map/ppermute | solution.py:18
  467.0 7.7 %collective-permute-start.5 = (f32[1,1,4,16384]{3,2,0,1:T(4,128)S(1)}, f32[1,1,4,16384]{3,2,0,1:T(4,128)S(1)}, u32[]{:S(2)}, u32[]{:S(2)}) collective-permute-start(f32[1,1,4,16384]{3,2,0,1:T(4,128)S(1)} %get-tuple-element.9), channel_id=1, source_target_pairs={{32,0},{64,32},{96,64},{128,96},{160,128},{192,160},{224,192},{33,... | collective-permute-start | bytes 786440 | tf_op jit(solution)/shard_map/ppermute | solution.py:20
  469.0 7.9 %collective-permute-start.6 = (f32[1,1,4,16384]{3,2,0,1:T(4,128)S(1)}, f32[1,1,4,16384]{3,2,0,1:T(4,128)S(1)}, u32[]{:S(2)}, u32[]{:S(2)}) collective-permute-start(f32[1,1,4,16384]{3,2,0,1:T(4,128)S(1)} %get-tuple-element.8), channel_id=1, source_target_pairs={{0,1},{1,2},{2,3},{3,4},{4,5},{5,6},{6,7},{7,8},{8,9},{9,10},{10,1... | collective-permute-start | bytes 786440 | tf_op jit(solution)/shard_map/ppermute | solution.py:18
  470.9 10.1 %collective-permute-start.7 = (f32[1,1,4,16384]{3,2,0,1:T(4,128)S(1)}, f32[1,1,4,16384]{3,2,0,1:T(4,128)S(1)}, u32[]{:S(2)}, u32[]{:S(2)}) collective-permute-start(f32[1,1,4,16384]{3,2,0,1:T(4,128)S(1)} %get-tuple-element.7), channel_id=1, source_target_pairs={{1,0},{2,1},{3,2},{4,3},{5,4},{6,5},{7,6},{8,7},{9,8},{10,9},{11,1... | collective-permute-start | bytes 786440 | tf_op jit(solution)/shard_map/ppermute | solution.py:20
Sparse Core Ops, SparseCore 0:
  12.7 211.5 reduce-scatter.1
